TPU v7x, 512 devices: a whole 4x4x16 slice. The times are simulated.
512 devices in a mesh: segment: 4 (over x_lo, core), ctx: 128 (over z, y, x_hi).
Axes of the slice: x: 4 (x_hi: 2, x_lo: 2; x = x_hi * 2 + x_lo), y: 4, z: 16, core: 2. Of those that a mesh axis runs over, the one named last changes fastest.
Arguments:
- queries: bfloat16 [4, 26624, 4096], P('segment', 'ctx'), may hold values from -8 to 8
- key_value_heads: bfloat16 [4, 26624, 1024], P('segment', 'ctx'), may hold values from -8 to 8
- doc_lengths: int32 [4, 64], P('segment'), may hold values from 1 to 1664, 26624 in all within a row
- norm_gain: float32 [4, 4096], P('segment'), may hold values from 0.5 to 1.5
Outputs:
- handed: bfloat16 [4, 26624, 4096], P('segment', 'ctx')
Inputs may be any that keep to these rules, and one draw needn't show every extreme that they name: `doc_lengths`: each row sums to 26624; its largest entry is 1664.
All inputs are finite; a program needn't handle non-finite values.
Results may differ from a plain program's by a relative error of at most 0.012.
The roundings to bfloat16 on the way count: a program that leaves them out, or rounds other values in their place, can miss the bound.
Values may be sent and summed in bfloat16 or wider, within the bound.
A program may use at most 64 MiB of HBM per device.

v0:
```python
import jax
import jax.numpy as jnp
from jax import lax
from jax.sharding import PartitionSpec as P

QUERY_HEADS = 32
KEY_VALUE_HEADS = 4
HEAD_SIZE = 128


def shifted(x, axis, by):
    peers = lax.axis_size(axis)
    pairs = [(i, i + by) for i in range(peers) if 0 <= i + by < peers]
    return lax.ppermute(x, axis, pairs)


def shifted_2(value, axis, steps):
    count = lax.axis_size(axis)
    pairs = [(source, (source + steps) % count) for source in range(count)]
    return lax.ppermute(value, axis, pairs)


def sign_table(size):
    rows = lax.broadcasted_iota(jnp.int32, (size, size), 0)
    cols = lax.broadcasted_iota(jnp.int32, (size, size), 1)
    parity = jnp.zeros((size, size), jnp.int32)
    for level in range(size.bit_length() - 1):
        parity = parity + rows // 2**level % 2 * (cols // 2**level % 2)
    return jnp.where(parity % 2 == 0, 1.0, -1.0).astype(jnp.float32)


def hadamard_rotate_heads(values, heads, lookup_table):
    token_rows = values.shape[0]
    width = lookup_table.shape[0]
    split = values.reshape(token_rows, heads, width)
    turned = jnp.einsum(
        "thd,de->the", split, lookup_table.astype(jnp.bfloat16), preferred_element_type=jnp.float32
    )
    return (turned * width ** (-0.5)).astype(jnp.bfloat16)


def doc_index(starts, positions):
    return (
        jnp.sum((starts[None, :] <= positions[:, None]).astype(jnp.int32), axis=1, dtype=jnp.int32)
        - 1
    )


def body(queries, key_value_heads, doc_lengths, norm_gain):
    lookup_table = sign_table(HEAD_SIZE)
    query_group = QUERY_HEADS // KEY_VALUE_HEADS
    scale = HEAD_SIZE ** (-0.5)
    token_rows = queries.shape[1]
    rotated_query = hadamard_rotate_heads(queries[0], QUERY_HEADS, lookup_table).reshape(
        token_rows, KEY_VALUE_HEADS, query_group, HEAD_SIZE
    )
    rotated_key_value = hadamard_rotate_heads(
        key_value_heads[0], 2 * KEY_VALUE_HEADS, lookup_table
    ).reshape(token_rows, 2 * KEY_VALUE_HEADS * HEAD_SIZE)
    lengths = doc_lengths[0]
    starts = jnp.cumsum(lengths, dtype=jnp.int32) - lengths
    reach = min(8, lax.axis_size("ctx") // 2)
    me = lax.axis_index("ctx")
    offsets = lax.broadcasted_iota(jnp.int32, (token_rows,), 0)
    q_pos = me * token_rows + offsets
    q_doc = doc_index(starts, q_pos)

    def attend(state, block_span, source):
        best, total, accum = state
        k_pos = source * token_rows + offsets
        k_doc = doc_index(starts, k_pos)
        allowed = (k_pos[None, :] <= q_pos[:, None]) & (k_doc[None, :] == q_doc[:, None])
        mask = allowed[None, :, None, :]
        key_rows = block_span[:, : KEY_VALUE_HEADS * HEAD_SIZE].reshape(
            token_rows, KEY_VALUE_HEADS, HEAD_SIZE
        )
        value_rows = block_span[:, KEY_VALUE_HEADS * HEAD_SIZE :].reshape(
            token_rows, KEY_VALUE_HEADS, HEAD_SIZE
        )
        scores = (
            jnp.einsum(
                "thgd,shd->htgs", rotated_query, key_rows, preferred_element_type=jnp.float32
            )
            * scale
        )
        scores = jnp.where(mask, scores, -jnp.inf)
        fresh = jnp.maximum(best, jnp.max(scores, axis=-1))
        anchor = jnp.where(fresh == -jnp.inf, 0.0, fresh)
        weights = jnp.where(mask, jnp.exp(scores - anchor[..., None]), 0.0)
        carried = jnp.exp(best - anchor)
        total = total * carried + jnp.sum(weights, axis=-1)
        product = jnp.einsum(
            "htgs,shd->htgd",
            weights.astype(jnp.bfloat16),
            value_rows,
            preferred_element_type=jnp.float32,
        )
        accum = accum * carried[..., None] + product
        return (fresh, total, accum)

    def visit(state, block_span, source):
        return attend(state, block_span, source)

    start_state = (
        jnp.full((KEY_VALUE_HEADS, token_rows, query_group), -jnp.inf, jnp.float32),
        jnp.zeros((KEY_VALUE_HEADS, token_rows, query_group), jnp.float32),
        jnp.zeros((KEY_VALUE_HEADS, token_rows, query_group, HEAD_SIZE), jnp.float32),
    )
    state = visit(start_state, rotated_key_value, me)

    def hop_step(step, carry):
        current, block_span = carry
        block_span = shifted(block_span, "ctx", 1)
        return (visit(current, block_span, me - step - 1), block_span)

    state, _ = lax.fori_loop(0, reach, hop_step, (state, rotated_key_value))
    best, total, accum = state
    heads_out = accum / total[..., None]
    restored = (
        jnp.einsum("htgd,de->thge", heads_out, lookup_table, precision=lax.Precision.HIGHEST)
        * scale
    )
    attended = restored.reshape(token_rows, QUERY_HEADS * HEAD_SIZE).astype(jnp.bfloat16)
    received = shifted_2(attended, "segment", 1).astype(jnp.float32)
    power = jnp.mean(received * received, axis=-1, keepdims=True)
    normed = received * lax.rsqrt(power + 1e-05) * norm_gain[0][None, :]
    return normed.astype(jnp.bfloat16)[None]


def solution(mesh):
    in_specs = (
        P("segment", "ctx", None),
        P("segment", "ctx", None),
        P("segment", None),
        P("segment", None),
    )
    out_specs = P("segment", "ctx", None)
    return jax.shard_map(body, mesh=mesh, in_specs=in_specs, out_specs=out_specs, check_vma=False)
```

profile of v0, /device:TPU:128, one launch (start us, length us, event | category | flops | bytes accessed | tf_op | source)
XLA Modules:
  0.0 364.2 jit_solution(10439930489536527970)
XLA Ops:
  7.3 1.7 fusion.22
  9.1 12.0 %fusion.24 = f32[4,208,8]{2,1,0:T(8,128)S(1)} fusion(f32[4,208,8,208]{3,2,1,0:T(8,128)S(1)} %get-tuple-element.387, f32[4,208,8]{2,1,0:T(8,128)S(1)} %compare_select_fusion.1, pred[208,208]{1,0:T(8,128)(4,1)S(1)} %compare_and_fusion.1), kind=kLoop, calls=%fused_computation.32 | loop fusion | flops 6915584 | bytes 5634304 | tf_op jit(solution)/shard_map/reduce_sum | solution.py:91
  21.9 5.1 %fusion.39 = f32[4,208,8,128]{3,2,1,0:T(8,128)} fusion(f32[4,208,8,208]{3,2,1,0:T(8,128)S(1)} %get-tuple-element.387, f32[4,208,8]{2,1,0:T(8,128)S(1)} %compare_select_fusion.1, pred[208,208]{1,0:T(8,128)(4,1)S(1)} %compare_and_fusion.1, f32[4,208,8]{2,1,0:T(8,128)S(1)} %get-tuple-element.384, bf16[208,4,128,1]{2,1,0,3:T(4,128)(2,1)S(1)} %bitcast.67), kind=kOutput, calls=%fused_computation.48 | convolution fusion | flops 362192896 | bytes 9255168 | tf_op jit(solution)/shard_map/htgs,shd->htgd/dot_general | solution.py:92
  27.0 304.7 %while.23 = (s32[]{:T(128)}, f32[4,208,8]{2,1,0:T(8,128)S(1)}, f32[4,208,8]{2,1,0:T(8,128)}, f32[4,208,8,128]{3,2,1,0:T(8,128)}, bf16[208,1024]{1,0:T(8,128)(2,1...) while((s32[]{:T(128)}, f32[4,208,8]{2,1,0:T(8,128)S(1)}, ...), condition=%wide.region_8.9_spmd.clone, body=%wide.region_4.8_spmd.clone.sunk | while | flops 728749184 | bytes 57929416 | solution.py:116
  27.0 4.9 %collective-permute-start = (bf16[208,1024]{1,0:T(8,128)(2,1)S(1)}, bf16[208,1024]{1,0:T(8,128)(2,1)S(1)}, u32[]{:S(2)}, u32[]{:S(2)}) collective-permute-start(bf16[208,1024]{1,0:T(8,128)(2,1)S(1)} %get-tuple-element.500), channel_id=1, source_target_pairs={{0,1},{1,2},{2,3},{3,4},{4,5},{5,6},{6,7},{7,8},{8,9},{9,10},{10,1... | collective-permute-start | bytes 1277960 | tf_op jit(solution)/shard_map/while/body/eval_jaxpr/ppermute | solution.py:14
  32.2 14.0 %collective-permute-done = bf16[208,1024]{1,0:T(8,128)(2,1)S(1)} collective-permute-done((bf16[208,1024]{1,0:T(8,128)(2,1)S(1)}, bf16[208,1024]{1,0:T(8,128)(2,1)S(1)}, u32[]{:S(2)}, u32[]{:S(2)}) %collective-permute-start) | collective-permute-done | bytes 426016 | tf_op jit(solution)/shard_map/while/body/eval_jaxpr/ppermute | solution.py:14
  46.3 1.6 fusion.120
  48.0 12.0 %fusion.121 = f32[4,208,8]{2,1,0:T(8,128)S(1)} fusion(f32[4,208,8,208]{3,2,1,0:T(8,128)S(1)} %get-tuple-element.478, f32[4,208,8]{2,1,0:T(8,128)S(1)} %get-tuple-element.479, pred[208,208]{1,0:T(8,128)(4,1)S(1)} %compare_and_fusion.9), kind=kLoop, calls=%fused_computation.6.clone.1 | loop fusion | flops 6915584 | bytes 5634304 | tf_op jit(solution)/shard_map/while/body/eval_jaxpr/reduce_sum | solution.py:91
  60.2 1.8 copy-done.2
  62.0 3.6 %multiply_add_fusion.5 = f32[4,208,8,128]{3,2,1,0:T(8,128)S(1)} fusion(f32[4,208,8,128]{3,2,1,0:T(8,128)S(1)} %copy-done.2, f32[4,208,8,208]{3,2,1,0:T(8,128)S(1)} %get-tuple-element.478, f32[4,208,8]{2,1,0:T(8,128)S(1)} %get-tuple-element.479, pred[208,208]{1,0:T(8,128)(4,1)S(1)} %compare_and_fusion.9, f32[4,208,8]{2,1,0:T(8,128)S(1)} %get-tuple-element.481, ...), kind=kOutput, calls=%fused_computation.8.clone.1 | convolution fusion | flops 363044864 | bytes 12663040 | tf_op jit(solution)/shard_map/while/body/eval_jaxpr/htgs,shd->htgd/dot_general | solution.py:92
  65.8 1.7 copy-done.3
  67.4 1.9 collective-permute-start
  69.6 16.1 %collective-permute-done = bf16[208,1024]{1,0:T(8,128)(2,1)S(1)} collective-permute-done((bf16[208,1024]{1,0:T(8,128)(2,1)S(1)}, bf16[208,1024]{1,0:T(8,128)(2,1)S(1)}, u32[]{:S(2)}, u32[]{:S(2)}) %collective-permute-start) | collective-permute-done | bytes 426016 | tf_op jit(solution)/shard_map/while/body/eval_jaxpr/ppermute | solution.py:14
  85.9 1.6 fusion.120
  87.6 12.0 %fusion.121 = f32[4,208,8]{2,1,0:T(8,128)S(1)} fusion(f32[4,208,8,208]{3,2,1,0:T(8,128)S(1)} %get-tuple-element.478, f32[4,208,8]{2,1,0:T(8,128)S(1)} %get-tuple-element.479, pred[208,208]{1,0:T(8,128)(4,1)S(1)} %compare_and_fusion.9), kind=kLoop, calls=%fused_computation.6.clone.1 | loop fusion | flops 6915584 | bytes 5634304 | tf_op jit(solution)/shard_map/while/body/eval_jaxpr/reduce_sum | solution.py:91
  99.8 1.8 copy-done.2
  101.6 3.6 %multiply_add_fusion.5 = f32[4,208,8,128]{3,2,1,0:T(8,128)S(1)} fusion(f32[4,208,8,128]{3,2,1,0:T(8,128)S(1)} %copy-done.2, f32[4,208,8,208]{3,2,1,0:T(8,128)S(1)} %get-tuple-element.478, f32[4,208,8]{2,1,0:T(8,128)S(1)} %get-tuple-element.479, pred[208,208]{1,0:T(8,128)(4,1)S(1)} %compare_and_fusion.9, f32[4,208,8]{2,1,0:T(8,128)S(1)} %get-tuple-element.481, ...), kind=kOutput, calls=%fused_computation.8.clone.1 | convolution fusion | flops 363044864 | bytes 12663040 | tf_op jit(solution)/shard_map/while/body/eval_jaxpr/htgs,shd->htgd/dot_general | solution.py:92
  105.3 1.7 copy-done.3
  107.0 1.9 collective-permute-start
  109.2 15.3 %collective-permute-done = bf16[208,1024]{1,0:T(8,128)(2,1)S(1)} collective-permute-done((bf16[208,1024]{1,0:T(8,128)(2,1)S(1)}, bf16[208,1024]{1,0:T(8,128)(2,1)S(1)}, u32[]{:S(2)}, u32[]{:S(2)}) %collective-permute-start) | collective-permute-done | bytes 426016 | tf_op jit(solution)/shard_map/while/body/eval_jaxpr/ppermute | solution.py:14
  124.6 1.6 fusion.120
  126.3 12.0 %fusion.121 = f32[4,208,8]{2,1,0:T(8,128)S(1)} fusion(f32[4,208,8,208]{3,2,1,0:T(8,128)S(1)} %get-tuple-element.478, f32[4,208,8]{2,1,0:T(8,128)S(1)} %get-tuple-element.479, pred[208,208]{1,0:T(8,128)(4,1)S(1)} %compare_and_fusion.9), kind=kLoop, calls=%fused_computation.6.clone.1 | loop fusion | flops 6915584 | bytes 5634304 | tf_op jit(solution)/shard_map/while/body/eval_jaxpr/reduce_sum | solution.py:91
  138.6 1.8 copy-done.2
  140.4 3.6 %multiply_add_fusion.5 = f32[4,208,8,128]{3,2,1,0:T(8,128)S(1)} fusion(f32[4,208,8,128]{3,2,1,0:T(8,128)S(1)} %copy-done.2, f32[4,208,8,208]{3,2,1,0:T(8,128)S(1)} %get-tuple-element.478, f32[4,208,8]{2,1,0:T(8,128)S(1)} %get-tuple-element.479, pred[208,208]{1,0:T(8,128)(4,1)S(1)} %compare_and_fusion.9, f32[4,208,8]{2,1,0:T(8,128)S(1)} %get-tuple-element.481, ...), kind=kOutput, calls=%fused_computation.8.clone.1 | convolution fusion | flops 363044864 | bytes 12663040 | tf_op jit(solution)/shard_map/while/body/eval_jaxpr/htgs,shd->htgd/dot_general | solution.py:92
  144.1 1.7 copy-done.3
  145.7 1.9 collective-permute-start
  147.9 14.4 %collective-permute-done = bf16[208,1024]{1,0:T(8,128)(2,1)S(1)} collective-permute-done((bf16[208,1024]{1,0:T(8,128)(2,1)S(1)}, bf16[208,1024]{1,0:T(8,128)(2,1)S(1)}, u32[]{:S(2)}, u32[]{:S(2)}) %collective-permute-start) | collective-permute-done | bytes 426016 | tf_op jit(solution)/shard_map/while/body/eval_jaxpr/ppermute | solution.py:14
  162.5 1.6 fusion.120
  164.2 12.0 %fusion.121 = f32[4,208,8]{2,1,0:T(8,128)S(1)} fusion(f32[4,208,8,208]{3,2,1,0:T(8,128)S(1)} %get-tuple-element.478, f32[4,208,8]{2,1,0:T(8,128)S(1)} %get-tuple-element.479, pred[208,208]{1,0:T(8,128)(4,1)S(1)} %compare_and_fusion.9), kind=kLoop, calls=%fused_computation.6.clone.1 | loop fusion | flops 6915584 | bytes 5634304 | tf_op jit(solution)/shard_map/while/body/eval_jaxpr/reduce_sum | solution.py:91
  176.4 1.8 copy-done.2
  178.2 3.6 %multiply_add_fusion.5 = f32[4,208,8,128]{3,2,1,0:T(8,128)S(1)} fusion(f32[4,208,8,128]{3,2,1,0:T(8,128)S(1)} %copy-done.2, f32[4,208,8,208]{3,2,1,0:T(8,128)S(1)} %get-tuple-element.478, f32[4,208,8]{2,1,0:T(8,128)S(1)} %get-tuple-element.479, pred[208,208]{1,0:T(8,128)(4,1)S(1)} %compare_and_fusion.9, f32[4,208,8]{2,1,0:T(8,128)S(1)} %get-tuple-element.481, ...), kind=kOutput, calls=%fused_computation.8.clone.1 | convolution fusion | flops 363044864 | bytes 12663040 | tf_op jit(solution)/shard_map/while/body/eval_jaxpr/htgs,shd->htgd/dot_general | solution.py:92
  181.9 1.7 copy-done.3
  183.6 1.9 collective-permute-start
  185.8 13.6 %collective-permute-done = bf16[208,1024]{1,0:T(8,128)(2,1)S(1)} collective-permute-done((bf16[208,1024]{1,0:T(8,128)(2,1)S(1)}, bf16[208,1024]{1,0:T(8,128)(2,1)S(1)}, u32[]{:S(2)}, u32[]{:S(2)}) %collective-permute-start) | collective-permute-done | bytes 426016 | tf_op jit(solution)/shard_map/while/body/eval_jaxpr/ppermute | solution.py:14
  199.5 1.6 fusion.120
  201.2 12.0 %fusion.121 = f32[4,208,8]{2,1,0:T(8,128)S(1)} fusion(f32[4,208,8,208]{3,2,1,0:T(8,128)S(1)} %get-tuple-element.478, f32[4,208,8]{2,1,0:T(8,128)S(1)} %get-tuple-element.479, pred[208,208]{1,0:T(8,128)(4,1)S(1)} %compare_and_fusion.9), kind=kLoop, calls=%fused_computation.6.clone.1 | loop fusion | flops 6915584 | bytes 5634304 | tf_op jit(solution)/shard_map/while/body/eval_jaxpr/reduce_sum | solution.py:91
  213.5 1.8 copy-done.2
  215.3 3.6 %multiply_add_fusion.5 = f32[4,208,8,128]{3,2,1,0:T(8,128)S(1)} fusion(f32[4,208,8,128]{3,2,1,0:T(8,128)S(1)} %copy-done.2, f32[4,208,8,208]{3,2,1,0:T(8,128)S(1)} %get-tuple-element.478, f32[4,208,8]{2,1,0:T(8,128)S(1)} %get-tuple-element.479, pred[208,208]{1,0:T(8,128)(4,1)S(1)} %compare_and_fusion.9, f32[4,208,8]{2,1,0:T(8,128)S(1)} %get-tuple-element.481, ...), kind=kOutput, calls=%fused_computation.8.clone.1 | convolution fusion | flops 363044864 | bytes 12663040 | tf_op jit(solution)/shard_map/while/body/eval_jaxpr/htgs,shd->htgd/dot_general | solution.py:92
  219.0 1.7 copy-done.3
  220.6 1.9 collective-permute-start
  222.8 13.6 %collective-permute-done = bf16[208,1024]{1,0:T(8,128)(2,1)S(1)} collective-permute-done((bf16[208,1024]{1,0:T(8,128)(2,1)S(1)}, bf16[208,1024]{1,0:T(8,128)(2,1)S(1)}, u32[]{:S(2)}, u32[]{:S(2)}) %collective-permute-start) | collective-permute-done | bytes 426016 | tf_op jit(solution)/shard_map/while/body/eval_jaxpr/ppermute | solution.py:14
  236.5 1.6 fusion.120
  238.2 12.0 %fusion.121 = f32[4,208,8]{2,1,0:T(8,128)S(1)} fusion(f32[4,208,8,208]{3,2,1,0:T(8,128)S(1)} %get-tuple-element.478, f32[4,208,8]{2,1,0:T(8,128)S(1)} %get-tuple-element.479, pred[208,208]{1,0:T(8,128)(4,1)S(1)} %compare_and_fusion.9), kind=kLoop, calls=%fused_computation.6.clone.1 | loop fusion | flops 6915584 | bytes 5634304 | tf_op jit(solution)/shard_map/while/body/eval_jaxpr/reduce_sum | solution.py:91
  250.5 1.8 copy-done.2
  252.3 3.6 %multiply_add_fusion.5 = f32[4,208,8,128]{3,2,1,0:T(8,128)S(1)} fusion(f32[4,208,8,128]{3,2,1,0:T(8,128)S(1)} %copy-done.2, f32[4,208,8,208]{3,2,1,0:T(8,128)S(1)} %get-tuple-element.478, f32[4,208,8]{2,1,0:T(8,128)S(1)} %get-tuple-element.479, pred[208,208]{1,0:T(8,128)(4,1)S(1)} %compare_and_fusion.9, f32[4,208,8]{2,1,0:T(8,128)S(1)} %get-tuple-element.481, ...), kind=kOutput, calls=%fused_computation.8.clone.1 | convolution fusion | flops 363044864 | bytes 12663040 | tf_op jit(solution)/shard_map/while/body/eval_jaxpr/htgs,shd->htgd/dot_general | solution.py:92
  256.0 1.7 copy-done.3
  257.6 1.9 collective-permute-start
  259.8 13.6 %collective-permute-done = bf16[208,1024]{1,0:T(8,128)(2,1)S(1)} collective-permute-done((bf16[208,1024]{1,0:T(8,128)(2,1)S(1)}, bf16[208,1024]{1,0:T(8,128)(2,1)S(1)}, u32[]{:S(2)}, u32[]{:S(2)}) %collective-permute-start) | collective-permute-done | bytes 426016 | tf_op jit(solution)/shard_map/while/body/eval_jaxpr/ppermute | solution.py:14
  273.5 1.6 fusion.120
  275.2 12.0 %fusion.121 = f32[4,208,8]{2,1,0:T(8,128)S(1)} fusion(f32[4,208,8,208]{3,2,1,0:T(8,128)S(1)} %get-tuple-element.478, f32[4,208,8]{2,1,0:T(8,128)S(1)} %get-tuple-element.479, pred[208,208]{1,0:T(8,128)(4,1)S(1)} %compare_and_fusion.9), kind=kLoop, calls=%fused_computation.6.clone.1 | loop fusion | flops 6915584 | bytes 5634304 | tf_op jit(solution)/shard_map/while/body/eval_jaxpr/reduce_sum | solution.py:91
  287.5 1.8 copy-done.2
  289.3 3.6 %multiply_add_fusion.5 = f32[4,208,8,128]{3,2,1,0:T(8,128)S(1)} fusion(f32[4,208,8,128]{3,2,1,0:T(8,128)S(1)} %copy-done.2, f32[4,208,8,208]{3,2,1,0:T(8,128)S(1)} %get-tuple-element.478, f32[4,208,8]{2,1,0:T(8,128)S(1)} %get-tuple-element.479, pred[208,208]{1,0:T(8,128)(4,1)S(1)} %compare_and_fusion.9, f32[4,208,8]{2,1,0:T(8,128)S(1)} %get-tuple-element.481, ...), kind=kOutput, calls=%fused_computation.8.clone.1 | convolution fusion | flops 363044864 | bytes 12663040 | tf_op jit(solution)/shard_map/while/body/eval_jaxpr/htgs,shd->htgd/dot_general | solution.py:92
  293.0 1.7 copy-done.3
  294.7 1.9 collective-permute-start
  296.8 13.6 %collective-permute-done = bf16[208,1024]{1,0:T(8,128)(2,1)S(1)} collective-permute-done((bf16[208,1024]{1,0:T(8,128)(2,1)S(1)}, bf16[208,1024]{1,0:T(8,128)(2,1)S(1)}, u32[]{:S(2)}, u32[]{:S(2)}) %collective-permute-start) | collective-permute-done | bytes 426016 | tf_op jit(solution)/shard_map/while/body/eval_jaxpr/ppermute | solution.py:14
  312.2 12.0 %fusion.121 = f32[4,208,8]{2,1,0:T(8,128)S(1)} fusion(f32[4,208,8,208]{3,2,1,0:T(8,128)S(1)} %get-tuple-element.478, f32[4,208,8]{2,1,0:T(8,128)S(1)} %get-tuple-element.479, pred[208,208]{1,0:T(8,128)(4,1)S(1)} %compare_and_fusion.9), kind=kLoop, calls=%fused_computation.6.clone.1 | loop fusion | flops 6915584 | bytes 5634304 | tf_op jit(solution)/shard_map/while/body/eval_jaxpr/reduce_sum | solution.py:91
  324.5 1.8 copy-done.2
  326.3 3.6 %multiply_add_fusion.5 = f32[4,208,8,128]{3,2,1,0:T(8,128)S(1)} fusion(f32[4,208,8,128]{3,2,1,0:T(8,128)S(1)} %copy-done.2, f32[4,208,8,208]{3,2,1,0:T(8,128)S(1)} %get-tuple-element.478, f32[4,208,8]{2,1,0:T(8,128)S(1)} %get-tuple-element.479, pred[208,208]{1,0:T(8,128)(4,1)S(1)} %compare_and_fusion.9, f32[4,208,8]{2,1,0:T(8,128)S(1)} %get-tuple-element.481, ...), kind=kOutput, calls=%fused_computation.8.clone.1 | convolution fusion | flops 363044864 | bytes 12663040 | tf_op jit(solution)/shard_map/while/body/eval_jaxpr/htgs,shd->htgd/dot_general | solution.py:92
  330.0 1.7 copy-done.3
  331.7 2.8 broadcast_divide_fusion
  334.5 3.2 fusion.44
  338.9 1.9 collective-permute-start.1
  340.8 21.2 %collective-permute-done.1 = bf16[208,4096]{1,0:T(8,128)(2,1)S(1)} collective-permute-done((bf16[208,4096]{1,0:T(8,128)(2,1)S(1)}, bf16[208,4096]{1,0:T(8,128)(2,1)S(1)}, u32[]{:S(2)}, u32[]{:S(2)}) %collective-permute-start.1) | collective-permute-done | bytes 1703968 | tf_op jit(solution)/shard_map/ppermute | solution.py:20
  362.5 1.7 fusion.42
  (182 shorter events, 17.6 us)
Async XLA Ops:
  3.7 1.5 copy-start.4
  27.0 19.2 %collective-permute-start = (bf16[208,1024]{1,0:T(8,128)(2,1)S(1)}, bf16[208,1024]{1,0:T(8,128)(2,1)S(1)}, u32[]{:S(2)}, u32[]{:S(2)}) collective-permute-start(bf16[208,1024]{1,0:T(8,128)(2,1)S(1)} %get-tuple-element.500), channel_id=1, source_target_pairs={{0,1},{1,2},{2,3},{3,4},{4,5},{5,6},{6,7},{7,8},{8,9},{9,10},{10,1... | collective-permute-start | bytes 1277960 | tf_op jit(solution)/shard_map/while/body/eval_jaxpr/ppermute | solution.py:14
  48.0 12.0 %copy-start = (f32[4,208,8]{2,1,0:T(8,128)S(1)}, f32[4,208,8]{2,1,0:T(8,128)}, u32[]{:S(2)}) copy-start(f32[4,208,8]{2,1,0:T(8,128)} %get-tuple-element.498) | copy-start | bytes 79876 | tf_op jit(solution)/shard_map/while
  59.9 2.1 copy-start.2
  60.2 5.5 %copy-start.1 = (f32[4,208,8]{2,1,0:T(8,128)}, f32[4,208,8]{2,1,0:T(8,128)S(1)}, u32[]{:S(2)}) copy-start(f32[4,208,8]{2,1,0:T(8,128)S(1)} %get-tuple-element.511) | copy-start | bytes 79876 | tf_op jit(solution)/shard_map/while
  65.7 1.7 copy-start.3
  67.4 18.3 %collective-permute-start = (bf16[208,1024]{1,0:T(8,128)(2,1)S(1)}, bf16[208,1024]{1,0:T(8,128)(2,1)S(1)}, u32[]{:S(2)}, u32[]{:S(2)}) collective-permute-start(bf16[208,1024]{1,0:T(8,128)(2,1)S(1)} %get-tuple-element.500), channel_id=1, source_target_pairs={{0,1},{1,2},{2,3},{3,4},{4,5},{5,6},{6,7},{7,8},{8,9},{9,10},{10,1... | collective-permute-start | bytes 1277960 | tf_op jit(solution)/shard_map/while/body/eval_jaxpr/ppermute | solution.py:14
  87.5 12.0 %copy-start = (f32[4,208,8]{2,1,0:T(8,128)S(1)}, f32[4,208,8]{2,1,0:T(8,128)}, u32[]{:S(2)}) copy-start(f32[4,208,8]{2,1,0:T(8,128)} %get-tuple-element.498) | copy-start | bytes 79876 | tf_op jit(solution)/shard_map/while
  99.5 2.1 copy-start.2
  99.8 5.5 %copy-start.1 = (f32[4,208,8]{2,1,0:T(8,128)}, f32[4,208,8]{2,1,0:T(8,128)S(1)}, u32[]{:S(2)}) copy-start(f32[4,208,8]{2,1,0:T(8,128)S(1)} %get-tuple-element.511) | copy-start | bytes 79876 | tf_op jit(solution)/shard_map/while
  105.3 1.7 copy-start.3
  107.0 17.4 %collective-permute-start = (bf16[208,1024]{1,0:T(8,128)(2,1)S(1)}, bf16[208,1024]{1,0:T(8,128)(2,1)S(1)}, u32[]{:S(2)}, u32[]{:S(2)}) collective-permute-start(bf16[208,1024]{1,0:T(8,128)(2,1)S(1)} %get-tuple-element.500), channel_id=1, source_target_pairs={{0,1},{1,2},{2,3},{3,4},{4,5},{5,6},{6,7},{7,8},{8,9},{9,10},{10,1... | collective-permute-start | bytes 1277960 | tf_op jit(solution)/shard_map/while/body/eval_jaxpr/ppermute | solution.py:14
  126.3 12.0 %copy-start = (f32[4,208,8]{2,1,0:T(8,128)S(1)}, f32[4,208,8]{2,1,0:T(8,128)}, u32[]{:S(2)}) copy-start(f32[4,208,8]{2,1,0:T(8,128)} %get-tuple-element.498) | copy-start | bytes 79876 | tf_op jit(solution)/shard_map/while
  138.2 2.1 copy-start.2
  138.5 5.5 %copy-start.1 = (f32[4,208,8]{2,1,0:T(8,128)}, f32[4,208,8]{2,1,0:T(8,128)S(1)}, u32[]{:S(2)}) copy-start(f32[4,208,8]{2,1,0:T(8,128)S(1)} %get-tuple-element.511) | copy-start | bytes 79876 | tf_op jit(solution)/shard_map/while
  144.0 1.7 copy-start.3
  145.7 16.6 %collective-permute-start = (bf16[208,1024]{1,0:T(8,128)(2,1)S(1)}, bf16[208,1024]{1,0:T(8,128)(2,1)S(1)}, u32[]{:S(2)}, u32[]{:S(2)}) collective-permute-start(bf16[208,1024]{1,0:T(8,128)(2,1)S(1)} %get-tuple-element.500), channel_id=1, source_target_pairs={{0,1},{1,2},{2,3},{3,4},{4,5},{5,6},{6,7},{7,8},{8,9},{9,10},{10,1... | collective-permute-start | bytes 1277960 | tf_op jit(solution)/shard_map/while/body/eval_jaxpr/ppermute | solution.py:14
  164.1 12.0 %copy-start = (f32[4,208,8]{2,1,0:T(8,128)S(1)}, f32[4,208,8]{2,1,0:T(8,128)}, u32[]{:S(2)}) copy-start(f32[4,208,8]{2,1,0:T(8,128)} %get-tuple-element.498) | copy-start | bytes 79876 | tf_op jit(solution)/shard_map/while
  176.1 2.1 copy-start.2
  176.4 5.5 %copy-start.1 = (f32[4,208,8]{2,1,0:T(8,128)}, f32[4,208,8]{2,1,0:T(8,128)S(1)}, u32[]{:S(2)}) copy-start(f32[4,208,8]{2,1,0:T(8,128)S(1)} %get-tuple-element.511) | copy-start | bytes 79876 | tf_op jit(solution)/shard_map/while
  181.9 1.7 copy-start.3
  183.6 15.7 %collective-permute-start = (bf16[208,1024]{1,0:T(8,128)(2,1)S(1)}, bf16[208,1024]{1,0:T(8,128)(2,1)S(1)}, u32[]{:S(2)}, u32[]{:S(2)}) collective-permute-start(bf16[208,1024]{1,0:T(8,128)(2,1)S(1)} %get-tuple-element.500), channel_id=1, source_target_pairs={{0,1},{1,2},{2,3},{3,4},{4,5},{5,6},{6,7},{7,8},{8,9},{9,10},{10,1... | collective-permute-start | bytes 1277960 | tf_op jit(solution)/shard_map/while/body/eval_jaxpr/ppermute | solution.py:14
  201.2 12.0 %copy-start = (f32[4,208,8]{2,1,0:T(8,128)S(1)}, f32[4,208,8]{2,1,0:T(8,128)}, u32[]{:S(2)}) copy-start(f32[4,208,8]{2,1,0:T(8,128)} %get-tuple-element.498) | copy-start | bytes 79876 | tf_op jit(solution)/shard_map/while
  213.1 2.1 copy-start.2
  213.4 5.5 %copy-start.1 = (f32[4,208,8]{2,1,0:T(8,128)}, f32[4,208,8]{2,1,0:T(8,128)S(1)}, u32[]{:S(2)}) copy-start(f32[4,208,8]{2,1,0:T(8,128)S(1)} %get-tuple-element.511) | copy-start | bytes 79876 | tf_op jit(solution)/shard_map/while
  218.9 1.7 copy-start.3
  220.6 15.7 %collective-permute-start = (bf16[208,1024]{1,0:T(8,128)(2,1)S(1)}, bf16[208,1024]{1,0:T(8,128)(2,1)S(1)}, u32[]{:S(2)}, u32[]{:S(2)}) collective-permute-start(bf16[208,1024]{1,0:T(8,128)(2,1)S(1)} %get-tuple-element.500), channel_id=1, source_target_pairs={{0,1},{1,2},{2,3},{3,4},{4,5},{5,6},{6,7},{7,8},{8,9},{9,10},{10,1... | collective-permute-start | bytes 1277960 | tf_op jit(solution)/shard_map/while/body/eval_jaxpr/ppermute | solution.py:14
  238.2 12.0 %copy-start = (f32[4,208,8]{2,1,0:T(8,128)S(1)}, f32[4,208,8]{2,1,0:T(8,128)}, u32[]{:S(2)}) copy-start(f32[4,208,8]{2,1,0:T(8,128)} %get-tuple-element.498) | copy-start | bytes 79876 | tf_op jit(solution)/shard_map/while
  250.1 2.1 copy-start.2
  250.4 5.5 %copy-start.1 = (f32[4,208,8]{2,1,0:T(8,128)}, f32[4,208,8]{2,1,0:T(8,128)S(1)}, u32[]{:S(2)}) copy-start(f32[4,208,8]{2,1,0:T(8,128)S(1)} %get-tuple-element.511) | copy-start | bytes 79876 | tf_op jit(solution)/shard_map/while
  255.9 1.7 copy-start.3
  257.6 15.7 %collective-permute-start = (bf16[208,1024]{1,0:T(8,128)(2,1)S(1)}, bf16[208,1024]{1,0:T(8,128)(2,1)S(1)}, u32[]{:S(2)}, u32[]{:S(2)}) collective-permute-start(bf16[208,1024]{1,0:T(8,128)(2,1)S(1)} %get-tuple-element.500), channel_id=1, source_target_pairs={{0,1},{1,2},{2,3},{3,4},{4,5},{5,6},{6,7},{7,8},{8,9},{9,10},{10,1... | collective-permute-start | bytes 1277960 | tf_op jit(solution)/shard_map/while/body/eval_jaxpr/ppermute | solution.py:14
  275.2 12.0 %copy-start = (f32[4,208,8]{2,1,0:T(8,128)S(1)}, f32[4,208,8]{2,1,0:T(8,128)}, u32[]{:S(2)}) copy-start(f32[4,208,8]{2,1,0:T(8,128)} %get-tuple-element.498) | copy-start | bytes 79876 | tf_op jit(solution)/shard_map/while
  287.1 2.1 copy-start.2
  287.4 5.5 %copy-start.1 = (f32[4,208,8]{2,1,0:T(8,128)}, f32[4,208,8]{2,1,0:T(8,128)S(1)}, u32[]{:S(2)}) copy-start(f32[4,208,8]{2,1,0:T(8,128)S(1)} %get-tuple-element.511) | copy-start | bytes 79876 | tf_op jit(solution)/shard_map/while
  292.9 1.7 copy-start.3
  294.7 15.7 %collective-permute-start = (bf16[208,1024]{1,0:T(8,128)(2,1)S(1)}, bf16[208,1024]{1,0:T(8,128)(2,1)S(1)}, u32[]{:S(2)}, u32[]{:S(2)}) collective-permute-start(bf16[208,1024]{1,0:T(8,128)(2,1)S(1)} %get-tuple-element.500), channel_id=1, source_target_pairs={{0,1},{1,2},{2,3},{3,4},{4,5},{5,6},{6,7},{7,8},{8,9},{9,10},{10,1... | collective-permute-start | bytes 1277960 | tf_op jit(solution)/shard_map/while/body/eval_jaxpr/ppermute | solution.py:14
  312.2 12.0 %copy-start = (f32[4,208,8]{2,1,0:T(8,128)S(1)}, f32[4,208,8]{2,1,0:T(8,128)}, u32[]{:S(2)}) copy-start(f32[4,208,8]{2,1,0:T(8,128)} %get-tuple-element.498) | copy-start | bytes 79876 | tf_op jit(solution)/shard_map/while
  324.2 2.1 copy-start.2
  324.4 5.5 %copy-start.1 = (f32[4,208,8]{2,1,0:T(8,128)}, f32[4,208,8]{2,1,0:T(8,128)S(1)}, u32[]{:S(2)}) copy-start(f32[4,208,8]{2,1,0:T(8,128)S(1)} %get-tuple-element.511) | copy-start | bytes 79876 | tf_op jit(solution)/shard_map/while
  329.9 1.7 copy-start.3
  338.1 24.4 %copy-start.5 = (f32[1,4096]{1,0:T(1,128)S(1)}, f32[1,4096]{1,0:T(1,128)}, u32[]{:S(2)}) copy-start(f32[1,4096]{1,0:T(1,128)} %param.9) | copy-start | bytes 49156
  338.9 23.1 %collective-permute-start.1 = (bf16[208,4096]{1,0:T(8,128)(2,1)S(1)}, bf16[208,4096]{1,0:T(8,128)(2,1)S(1)}, u32[]{:S(2)}, u32[]{:S(2)}) collective-permute-start(bf16[208,4096]{1,0:T(8,128)(2,1)S(1)} %bitcast.60), channel_id=1, source_target_pairs={{0,128},{128,256},{256,384},{384,0},{1,129},{129,257},{257,385},{3... | collective-permute-start | bytes 5111816 | tf_op jit(solution)/shard_map/ppermute | solution.py:20
where the time goes:
time: 365 us; the launch traced here: 364 us
  waiting for transfers between devices  135 us (37%)
  other arithmetic  120 us (33%)
  matrix products  53.7 us (15%)
  local copies, waits for them, and re-layouts  34.1 us (9%)
  starting transfers between devices  20.2 us (6%)
    ppermute x8, waiting for transfers between devices, shifted(): return lax.ppermute(x, axis, pairs)  114 us
    reduce_sum x9, other arithmetic, attend(): total = total * carried + jnp.sum(weights, axis=-1)  108 us
    dot_general x9, matrix products, attend(): jnp.einsum('htgs,shd->htgd', weights.astype(jnp.bfloat16), value_rows, pr...  34.3 us
    while x80, local copies, waits for them, and re-layouts  28.4 us
    ppermute x1, waiting for transfers between devices, shifted_2(): return lax.ppermute(value, axis, pairs)  21.2 us
    ppermute x8, starting transfers between devices, shifted(): return lax.ppermute(x, axis, pairs)  18.3 us
    dot_general x9, matrix products, attend(): jnp.einsum('thgd,shd->htgs', rotated_query, key_rows, preferred_element_t...  14.2 us
  transfers between devices with their start and end apart: 9, of which 9 were waited for; matrix products, arithmetic and copies ran while one was open for 1% of the time, Pallas kernels for 0%

commit v1 on v0

v1 whole, which is shorter than its diff:
```python
import functools

import jax
import jax.numpy as jnp
import numpy as np
from jax import lax
from jax.experimental import pallas as pl
from jax.experimental.pallas import tpu as pltpu
from jax.sharding import PartitionSpec as P

QUERY_HEADS = 32
KEY_VALUE_HEADS = 4
HEAD = 128
GROUP = QUERY_HEADS // KEY_VALUE_HEADS
NDOC = 64
SPAN = 8
SLOTS = SPAN + 3
MESH = pl.DeviceIdType.MESH
PV, ZO, ZP, D2O, D2P, D4O, D4P, D6O, D6P, RELAY = range(10)
SENDS = 10
CHUNK = 256
LOW = -1e30


def hadamard(size):
    rows = lax.broadcasted_iota(jnp.int32, (size, size), 0)
    cols = lax.broadcasted_iota(jnp.int32, (size, size), 1)
    both = rows & cols
    both = both ^ (both >> 4)
    both = both ^ (both >> 2)
    both = both ^ (both >> 1)
    return jnp.where((both & 1) == 0, 1.0, -1.0).astype(jnp.bfloat16)


def interleave(*parts):
    parts = list(parts)
    while parts:
        for part in list(parts):
            try:
                next(part)
            except StopIteration:
                parts.remove(part)


def kernel(
    tok, planes, sections,
    q_hbm, kv_ref, len_ref, gain_ref, out_ref,
    q_ref, kvb, qr, scores, tops, tri, att, got, lens,
    q_sem, send_sem, recv_sem, att_send, att_recv,
):
    width = -(-((SPAN + 1) * tok) // 128) * 128
    scale = HEAD ** (-0.5)
    c = lax.axis_index("ctx")
    s = lax.axis_index("segment")
    h = lax.rem(c, 2)
    y = lax.rem(c // 2, 4)
    z = c // 8
    e = 1 - 2 * h
    up = lax.rem(z + 1, planes)
    down = lax.rem(z + planes - 1, planes)
    right = lax.rem(y + 1, 4)
    left = lax.rem(y + 3, 4)

    def at(zz, yy, hh):
        return zz * 8 + yy * 2 + hh

    partner = {"ctx": at(z, y, 1 - h)}
    above = {"ctx": at(up, y, h)}
    below = {"ctx": at(down, y, h)}
    to_right = {"ctx": at(z, right, h)}
    to_left = {"ctx": at(z, left, h)}
    after = {"segment": lax.rem(s + 1, sections)}
    before = {"segment": lax.rem(s + sections - 1, sections)}

    q_copy = pltpu.make_async_copy(q_hbm, q_ref, q_sem)
    q_copy.start()
    barrier = pltpu.get_barrier_semaphore()
    for who in (partner, below, above, to_right, to_left, before, after):
        pl.semaphore_signal(barrier, inc=1, device_id=who, device_id_type=MESH)

    had = hadamard(HEAD)

    def turn(x):
        return (jnp.dot(x, had, preferred_element_type=jnp.float32) * scale).astype(jnp.bfloat16)

    def rows(slot):
        return pl.ds(pl.multiple_of(slot * tok, 16), tok)

    def send(g, k, src, dst, role, who):
        return pltpu.make_async_remote_copy(
            src_ref=kvb.at[g, rows(src), :],
            dst_ref=kvb.at[g, rows(dst), :],
            send_sem=send_sem.at[g, k],
            recv_sem=recv_sem.at[g, role],
            device_id=who,
            device_id_type=MESH,
        )

    def arrived(g, role):
        pltpu.make_async_remote_copy(
            src_ref=kvb.at[g, rows(0), :],
            dst_ref=kvb.at[g, rows(0), :],
            send_sem=send_sem.at[g, 0],
            recv_sem=recv_sem.at[g, role],
            device_id=partner,
            device_id_type=MESH,
        ).wait_recv()

    pv = SPAN + e
    pp = lax.rem(e + 10, 10)

    def table(g, yy):
        entries = {None: [], PV: [], ZO: [], ZP: [], D2O: [], D2P: [], D6O: [], D6P: [], RELAY: []}
        count = [3]

        def add(when, src, dst, role, who):
            entries[when].append(functools.partial(send, g, count[0], src, dst, role, who))
            count[0] += 1

        v_dirs = {0: (1, 3), 1: (1,), 2: (1,), 3: ()}[yy]
        p_dirs = {0: (), 1: (-1,), 2: (-1,), 3: (-3, -1)}[yy]
        for d in v_dirs:
            who = to_right if d == 1 else to_left
            own, pair = (D6O, D6P) if d == 1 else (D2O, D2P)
            add(None, SPAN, SPAN - 2 * d, own, who)
            add(PV, pv, SPAN - 2 * d + e, pair, who)
        for d in p_dirs:
            who = to_right if d == -3 else to_left
            own, pair = (D6O, D6P) if d == -3 else (D2O, D2P)
            add(ZO, 0, -2 * d, own, who)
            add(ZP, pp, -2 * d + e, pair, who)
        if yy == 0:
            add(D6O, 6, 4, D4O, to_right)
            add(D2O, 2, 10, RELAY, below)
            add(RELAY, 10, 4, D4O, to_left)
        if yy == 1:
            add(D6O, 6, 4, D4O, to_right)
            add(D2P, 2 + e, 4 + e, D4P, to_left)
        if yy == 2:
            add(D6P, 6 + e, 4 + e, D4P, to_right)
            add(D2P, 2 + e, 4 + e, D4P, to_left)
        if yy == 3:
            add(D2P, 2 + e, 4 + e, D4P, to_left)
            add(D6O, 6, 10, RELAY, above)
            add(RELAY, 10, 4, D4O, to_right)
        return entries

    def common(g):
        return (
            functools.partial(send, g, 0, SPAN, SPAN - e, PV, partner),
            functools.partial(send, g, 1, SPAN, 0, ZO, above),
            functools.partial(send, g, 2, pv, pp, ZP, above),
        )

    def first(g):
        across, lift, _ = common(g)
        across().start()
        for yy in (0, 1, 2):

            @pl.when(y == yy)
            def _(yy=yy):
                for copy in table(g, yy)[None]:
                    copy().start()

        lift().start()

    def pass_on(g, role):
        arrived(g, role)
        if role == PV:
            common(g)[2]().start()
        for yy in range(4):
            if table(g, yy)[role]:

                @pl.when(y == yy)
                def _(yy=yy):
                    for copy in table(g, yy)[role]:
                        copy().start()

    order = {0: (D2O, D6O, RELAY), 1: (D6O, D2P), 2: (D6P, D2P), 3: (D6O, D2P, RELAY)}

    def later(g, which):
        for yy in range(4):
            if which < len(order[yy]):

                @pl.when(y == yy)
                def _(yy=yy):
                    role = order[yy][which]
                    arrived(g, role)
                    for copy in table(g, yy)[role]:
                        copy().start()

    def complete(g):
        for yy in range(4):

            @pl.when(y == yy)
            def _(yy=yy):
                for role in (D2O, D2P, D4O, D4P, D6O, D6P):
                    if role not in order[yy]:
                        arrived(g, role)

    def drain(g):
        for copy in common(g):
            copy().wait_send()
        for yy in range(4):

            @pl.when(y == yy)
            def _(yy=yy):
                for copies in table(g, yy).values():
                    for copy in copies:
                        copy().wait_send()

    for g in range(KEY_VALUE_HEADS):
        kvb[g, SPAN * tok : (SPAN + 1) * tok, :HEAD] = turn(kv_ref[:, g * HEAD : (g + 1) * HEAD])
        kvb[g, SPAN * tok : (SPAN + 1) * tok, HEAD:] = turn(
            kv_ref[:, (KEY_VALUE_HEADS + g) * HEAD : (KEY_VALUE_HEADS + g + 1) * HEAD]
        )

    pl.semaphore_wait(barrier, 7)
    first(0)
    first(1)

    lens[...] = jnp.zeros_like(lens)
    lens[0:1, 0:NDOC] = len_ref[...]
    lane = lax.broadcasted_iota(jnp.int32, (8, 128), 1)
    ends = lens[...]
    for step in (1, 2, 4, 8, 16, 32, 64):
        ends = ends + jnp.where(lane >= step, pltpu.roll(ends, step, 1), 0)
    starts = (ends - lens[...])[0:1, :]
    row = lax.broadcasted_iota(jnp.int32, (tok, 128), 0)
    begun = jnp.where(starts <= row + c * tok, starts, -1)
    tri[...] = jnp.broadcast_to(
        jnp.max(begun, axis=1, keepdims=True) - c * tok + SPAN * tok, (tok, 128)
    )

    q_copy.wait()
    for i in range(QUERY_HEADS):
        qr[i * tok : (i + 1) * tok, :] = turn(q_ref[:, i * HEAD : (i + 1) * HEAD])

    def score(g, slot):
        count = GROUP * tok
        q = qr[g * count : (g + 1) * count, :]
        low = tri[...]
        lanes = lax.broadcasted_iota(jnp.int32, (1, 128), 1)
        most = [jnp.full((tok, 128), LOW, jnp.float32) for _ in range(GROUP)]
        for c0 in range(0, width, CHUNK):
            n = min(CHUNK, width - c0)
            k = kvb[g, c0 : c0 + n, :HEAD]
            part = lax.dot_general(
                q, k, (((1,), (1,)), ((), ())), preferred_element_type=jnp.float32
            )
            for t in range(0, n, 128):
                place = lanes + (c0 + t)
                ok = place >= low
                if c0 + t + 127 >= SPAN * tok:
                    ok = ok & (place <= row + SPAN * tok)
                for a in range(GROUP):
                    one = jnp.where(ok, part[a * tok : (a + 1) * tok, t : t + 128], LOW)
                    scores[slot, a * tok : (a + 1) * tok, c0 + t : c0 + t + 128] = one
                    most[a] = jnp.maximum(most[a], one)
            yield
        for a in range(GROUP):
            tops[slot, a * tok : (a + 1) * tok] = jnp.broadcast_to(
                jnp.max(most[a], axis=1, keepdims=True), (tok, 128)
            )

    def mix(g, slot):
        acc = jnp.zeros((GROUP * tok, 2 * HEAD), jnp.float32)
        ones = jnp.ones((CHUNK, HEAD), jnp.bfloat16)
        top = tops[slot]
        for c0 in range(0, width, CHUNK):
            n = min(CHUNK, width - c0)
            p = jnp.concatenate(
                [
                    jnp.exp2(
                        (scores[slot, :, c0 + t : c0 + t + 128] - top) * (scale * np.log2(np.e))
                    ).astype(jnp.bfloat16)
                    for t in range(0, n, 128)
                ],
                axis=1,
            )
            v = jnp.concatenate([kvb[g, c0 : c0 + n, HEAD:], ones[:n]], axis=1)
            acc = acc + jnp.dot(p, v, preferred_element_type=jnp.float32)
            yield
        mean = acc[:, :HEAD] / acc[:, HEAD:]
        big = mean.astype(jnp.bfloat16)
        small = (mean - big.astype(jnp.float32)).astype(jnp.bfloat16)
        back = jnp.dot(big, had, preferred_element_type=jnp.float32) + jnp.dot(
            small, had, preferred_element_type=jnp.float32
        )
        back = (back * scale).astype(jnp.bfloat16)
        for a in range(GROUP):
            att[g, :, a * HEAD : (a + 1) * HEAD] = back[a * tok : (a + 1) * tok]

    def ship(g):
        return pltpu.make_async_remote_copy(
            src_ref=att.at[g],
            dst_ref=got.at[g],
            send_sem=att_send.at[g],
            recv_sem=att_recv.at[g],
            device_id=after,
            device_id_type=MESH,
        )

    last = KEY_VALUE_HEADS - 1
    pass_on(0, PV)
    pass_on(0, ZO)
    pass_on(1, PV)
    pass_on(1, ZO)
    pass_on(0, ZP)
    later(0, 0)
    first(2)
    later(0, 1)
    pass_on(1, ZP)
    pass_on(2, PV)
    pass_on(2, ZO)
    later(0, 2)
    complete(0)
    later(1, 0)
    first(3)

    def during(g):
        yield
        if g + 1 <= last:
            later(g + 1, 1)
        if g + 2 <= last:
            pass_on(g + 2, ZP)
        if g + 3 <= last:
            pass_on(g + 3, PV)
            pass_on(g + 3, ZO)
        yield
        yield
        if g + 1 <= last:
            later(g + 1, 2)
        if g + 2 <= last:
            later(g + 2, 0)

    interleave(score(0, 0), during(0))
    for g in range(1, KEY_VALUE_HEADS):
        complete(g)
        interleave(score(g, g % 2), mix(g - 1, (g - 1) % 2), during(g))
        ship(g - 1).start()
    interleave(mix(last, last % 2))
    ship(last).start()

    for g in range(KEY_VALUE_HEADS):
        drain(g)
    for g in range(KEY_VALUE_HEADS):
        ship(g).wait()

    many = QUERY_HEADS * HEAD

    def finish(i, _):
        r = pl.ds(pl.multiple_of(i * 16, 16), 16)
        x = [got[g, r, :].astype(jnp.float32) for g in range(KEY_VALUE_HEADS)]
        power = sum(jnp.sum(v * v, axis=1, keepdims=True) for v in x) / many
        factor = lax.rsqrt(power + 1e-05)
        step = GROUP * HEAD
        for g in range(KEY_VALUE_HEADS):
            out_ref[r, g * step : (g + 1) * step] = (
                x[g] * factor * gain_ref[:, g * step : (g + 1) * step]
            ).astype(jnp.bfloat16)
        return 0

    lax.fori_loop(0, tok // 16, finish, 0)


def solution(mesh):
    planes = mesh.shape["ctx"] // 8
    sections = mesh.shape["segment"]

    def body(queries, key_value_heads, doc_lengths, norm_gain):
        tok = queries.shape[1]
        width = -(-((SPAN + 1) * tok) // 128) * 128
        vmem = pl.BlockSpec(memory_space=pltpu.VMEM)
        bf16, f32 = jnp.bfloat16, jnp.float32
        out = pl.pallas_call(
            functools.partial(kernel, tok, planes, sections),
            out_shape=jax.ShapeDtypeStruct((tok, QUERY_HEADS * HEAD), bf16),
            in_specs=[pl.BlockSpec(memory_space=pl.ANY), vmem, vmem, vmem],
            out_specs=vmem,
            scratch_shapes=[
                pltpu.VMEM((tok, QUERY_HEADS * HEAD), bf16),
                pltpu.VMEM((KEY_VALUE_HEADS, SLOTS * tok, 2 * HEAD), bf16),
                pltpu.VMEM((QUERY_HEADS * tok, HEAD), bf16),
                pltpu.VMEM((2, GROUP * tok, width), f32),
                pltpu.VMEM((2, GROUP * tok, 128), f32),
                pltpu.VMEM((tok, 128), jnp.int32),
                pltpu.VMEM((KEY_VALUE_HEADS, tok, GROUP * HEAD), bf16),
                pltpu.VMEM((KEY_VALUE_HEADS, tok, GROUP * HEAD), bf16),
                pltpu.VMEM((8, 128), jnp.int32),
                pltpu.SemaphoreType.DMA,
                pltpu.SemaphoreType.DMA((KEY_VALUE_HEADS, SENDS)),
                pltpu.SemaphoreType.DMA((KEY_VALUE_HEADS, 10)),
                pltpu.SemaphoreType.DMA((KEY_VALUE_HEADS,)),
                pltpu.SemaphoreType.DMA((KEY_VALUE_HEADS,)),
            ],
            compiler_params=pltpu.CompilerParams(
                collective_id=0, has_side_effects=True, vmem_limit_bytes=62 * 2**20
            ),
        )(queries[0], key_value_heads[0], doc_lengths, norm_gain)
        return out[None]

    in_specs = (
        P("segment", "ctx", None),
        P("segment", "ctx", None),
        P("segment", None),
        P("segment", None),
    )
    return jax.shard_map(
        body, mesh=mesh, in_specs=in_specs, out_specs=P("segment", "ctx", None), check_vma=False
    )
```

time: 365 us -> 79.9 us (0.22)
  the two profiles are of different devices: /device:TPU:128 before, /device:TPU:1 now
where the time goes in v1:
time: 79.9 us; the launch traced here: 79.7 us
  Pallas kernels  76.9 us (96%)
  local copies, waits for them, and re-layouts  2.81 us (4%)
    pallas_call x1, Pallas kernels, body(): pl.pallas_call(functools.partial(kernel, tok, planes, sections), out_shap...  76.9 us
    unnamed x1, local copies, waits for them, and re-layouts  2.81 us

profile of v1, /device:TPU:1, one launch (start us, length us, event | category | flops | bytes accessed | tf_op | source)
XLA Modules:
  0.0 79.7 jit_solution(3239939761317451489)
XLA Ops:
  0.0 76.9 %shard_map.46 = bf16[208,4096]{1,0:T(8,128)(2,1)} custom-call(bf16[208,4096]{1,0:T(8,128)(2,1)} %bitcast.4, bf16[208,1024]{1,0:T(8,128)(2,1)} %bitcast.5, s32[1,64]{1,0:T(1,128)} %len_ref.1, f32[1,4096]{1,0:T(1,128)} %gain_ref.1), custom_call_target="tpu_custom_call" | custom-call | tf_op jit(solution)/shard_map/pallas_call | solution.py:376
  76.9 2.8 %copy.6 = bf16[1,208,4096]{2,1,0:T(8,128)(2,1)} copy(bf16[1,208,4096]{2,1,0:T(8,128)(2,1)} %bitcast.3) | data formatting | bytes 3407872

commit v2 on v1

v2 whole, which is shorter than its diff:
```python
import functools

import jax
import jax.numpy as jnp
import numpy as np
from jax import lax
from jax.experimental import pallas as pl
from jax.experimental.pallas import tpu as pltpu
from jax.sharding import PartitionSpec as P

QUERY_HEADS = 32
KEY_VALUE_HEADS = 4
HEAD = 128
GROUP = QUERY_HEADS // KEY_VALUE_HEADS
NDOC = 64
SPAN = 8
SLOTS = SPAN + 3
MESH = pl.DeviceIdType.MESH
PV, ZO, ZP, D2O, D2P, D4O, D4P, D6O, D6P, RELAY = range(10)
SENDS = 10
CHUNK = 256
TILE = 128
HALF = GROUP // 2
LOW = -1e30


def hadamard(size):
    rows = lax.broadcasted_iota(jnp.int32, (size, size), 0)
    cols = lax.broadcasted_iota(jnp.int32, (size, size), 1)
    both = rows & cols
    both = both ^ (both >> 4)
    both = both ^ (both >> 2)
    both = both ^ (both >> 1)
    return jnp.where((both & 1) == 0, 1.0, -1.0).astype(jnp.bfloat16)


def kernel(
    tok, planes, sections,
    q_hbm, kv_ref, len_ref, got,
    q_ref, kvb, qr, scores, sums, tops, fade, tri, att, lens,
    q_sem, send_sem, recv_sem, att_send, att_recv,
):
    width = -(-((SPAN + 1) * tok) // 128) * 128
    scale = HEAD ** (-0.5)
    c = lax.axis_index("ctx")
    s = lax.axis_index("segment")
    h = lax.rem(c, 2)
    y = lax.rem(c // 2, 4)
    z = c // 8
    e = 1 - 2 * h
    up = lax.rem(z + 1, planes)
    down = lax.rem(z + planes - 1, planes)
    right = lax.rem(y + 1, 4)
    left = lax.rem(y + 3, 4)

    def at(zz, yy, hh):
        return zz * 8 + yy * 2 + hh

    partner = {"ctx": at(z, y, 1 - h)}
    above = {"ctx": at(up, y, h)}
    below = {"ctx": at(down, y, h)}
    to_right = {"ctx": at(z, right, h)}
    to_left = {"ctx": at(z, left, h)}
    after = {"segment": lax.rem(s + 1, sections)}
    before = {"segment": lax.rem(s + sections - 1, sections)}

    q_copy = pltpu.make_async_copy(q_hbm, q_ref, q_sem)
    q_copy.start()
    barrier = pltpu.get_barrier_semaphore()
    for who in (partner, below, above, to_right, to_left, before, after):
        pl.semaphore_signal(barrier, inc=1, device_id=who, device_id_type=MESH)

    had = hadamard(HEAD)

    def turn(x):
        return (jnp.dot(x, had, preferred_element_type=jnp.float32) * scale).astype(jnp.bfloat16)

    def rows(slot):
        return pl.ds(pl.multiple_of(slot * tok, 16), tok)

    def send(g, k, src, dst, role, who):
        return pltpu.make_async_remote_copy(
            src_ref=kvb.at[g, rows(src), :],
            dst_ref=kvb.at[g, rows(dst), :],
            send_sem=send_sem.at[g, k],
            recv_sem=recv_sem.at[g, role],
            device_id=who,
            device_id_type=MESH,
        )

    def arrived(g, role):
        pltpu.make_async_remote_copy(
            src_ref=kvb.at[g, rows(0), :],
            dst_ref=kvb.at[g, rows(0), :],
            send_sem=send_sem.at[g, 0],
            recv_sem=recv_sem.at[g, role],
            device_id=partner,
            device_id_type=MESH,
        ).wait_recv()

    pv = SPAN + e
    pp = lax.rem(e + 10, 10)

    def table(g, yy):
        entries = {None: [], PV: [], ZO: [], ZP: [], D2O: [], D2P: [], D6O: [], D6P: [], RELAY: []}
        count = [3]

        def add(when, src, dst, role, who):
            entries[when].append(functools.partial(send, g, count[0], src, dst, role, who))
            count[0] += 1

        v_dirs = {0: (1, 3), 1: (1,), 2: (1,), 3: ()}[yy]
        p_dirs = {0: (), 1: (-1,), 2: (-1,), 3: (-3, -1)}[yy]
        for d in v_dirs:
            who = to_right if d == 1 else to_left
            own, pair = (D6O, D6P) if d == 1 else (D2O, D2P)
            add(None, SPAN, SPAN - 2 * d, own, who)
            add(PV, pv, SPAN - 2 * d + e, pair, who)
        for d in p_dirs:
            who = to_right if d == -3 else to_left
            own, pair = (D6O, D6P) if d == -3 else (D2O, D2P)
            add(ZO, 0, -2 * d, own, who)
            add(ZP, pp, -2 * d + e, pair, who)
        if yy == 0:
            add(D6O, 6, 4, D4O, to_right)
            add(D2O, 2, 10, RELAY, below)
            add(RELAY, 10, 4, D4O, to_left)
        if yy == 1:
            add(D6O, 6, 4, D4O, to_right)
            add(D2P, 2 + e, 4 + e, D4P, to_left)
        if yy == 2:
            add(D6P, 6 + e, 4 + e, D4P, to_right)
            add(D2P, 2 + e, 4 + e, D4P, to_left)
        if yy == 3:
            add(D2P, 2 + e, 4 + e, D4P, to_left)
            add(D6O, 6, 10, RELAY, above)
            add(RELAY, 10, 4, D4O, to_right)
        return entries

    def common(g):
        return (
            functools.partial(send, g, 0, SPAN, SPAN - e, PV, partner),
            functools.partial(send, g, 1, SPAN, 0, ZO, above),
            functools.partial(send, g, 2, pv, pp, ZP, above),
        )

    def only(places, run):
        for yy in places:
            pl.when(y == yy)(functools.partial(run, yy))

    def across(g):
        common(g)[0]().start()

    def own(g):
        def run(yy):
            for copy in table(g, yy)[None]:
                copy().start()

        only((0, 1, 2), run)
        common(g)[1]().start()

    def pass_on(g, role, places=(0, 1, 2, 3)):
        def run(yy):
            for copy in table(g, yy)[role]:
                copy().start()

        arrived(g, role)
        if role == PV:
            common(g)[2]().start()
        only([yy for yy in places if table(g, yy)[role]], run)

    own_roles = {0: (D2O, D6O), 1: (D6O,), 3: (D6O,)}
    near_roles = {1: (D6O,), 3: (D6O,)}
    far_roles = {0: (D2O, D6O)}
    pair_roles = {1: (D2P,), 2: (D6P, D2P), 3: (D2P,)}
    relay_roles = {0: (RELAY,), 3: (RELAY,)}

    def onward(g, roles):
        def run(yy):
            for role in roles[yy]:
                arrived(g, role)
                for copy in table(g, yy)[role]:
                    copy().start()

        only(roles, run)

    def complete(g):
        def run(yy):
            seen = own_roles.get(yy, ()) + pair_roles.get(yy, ())
            for role in (D2O, D2P, D6O, D6P):
                if role not in seen:
                    arrived(g, role)

        only(range(4), run)

    def complete_last(g):
        arrived(g, D4O)
        arrived(g, D4P)

    def drain(g):
        for copy in common(g):
            copy().wait_send()
        for yy in range(4):

            @pl.when(y == yy)
            def _(yy=yy):
                for copies in table(g, yy).values():
                    for copy in copies:
                        copy().wait_send()

    def block(run, *args):
        pl.when(c >= 0)(functools.partial(run, *args))

    def rotate(g):
        kvb[g, SPAN * tok : (SPAN + 1) * tok, :HEAD] = turn(kv_ref[:, g * HEAD : (g + 1) * HEAD])
        kvb[g, SPAN * tok : (SPAN + 1) * tok, HEAD:] = turn(
            kv_ref[:, (KEY_VALUE_HEADS + g) * HEAD : (KEY_VALUE_HEADS + g + 1) * HEAD]
        )

    block(rotate, 0)
    block(rotate, 1)
    pl.semaphore_wait(barrier, 7)
    for g in (0, 1):
        across(g)
        own(g)
    block(rotate, 2)
    block(rotate, 3)
    across(2)
    across(3)

    lens[...] = jnp.zeros_like(lens)
    lens[0:1, 0:NDOC] = len_ref[...]
    lane = lax.broadcasted_iota(jnp.int32, (8, 128), 1)
    ends = lens[...]
    for step in (1, 2, 4, 8, 16, 32, 64):
        ends = ends + jnp.where(lane >= step, pltpu.roll(ends, step, 1), 0)
    starts = (ends - lens[...])[0:1, :]
    row = lax.broadcasted_iota(jnp.int32, (tok, 128), 0)
    begun = jnp.where(starts <= row + c * tok, starts, -1)
    tri[...] = jnp.broadcast_to(
        jnp.max(begun, axis=1, keepdims=True) - c * tok + SPAN * tok, (tok, 128)
    )

    q_copy.wait()

    def rotate_queries(i):
        for a in range(i * GROUP, (i + 1) * GROUP):
            qr[a * tok : (a + 1) * tok, :] = turn(q_ref[:, a * HEAD : (a + 1) * HEAD])

    tiles = width // TILE
    late = list(range((SPAN // 2 - 1) * tok // TILE, -(-(SPAN // 2 + 2) * tok // TILE)))
    before_late, after_late = list(range(late[0])), list(range(late[-1] + 1, tiles))

    def paired(some):
        return [some[i : i + 2] for i in range(0, len(some), 2)]

    early_pairs = paired(before_late) + paired(after_late)
    late_pairs = paired(late)
    factor = scale * np.log2(np.e)

    def score(g, pairs):
        count = GROUP * tok
        q = qr[g * count : (g + 1) * count, :]
        low = tri[...]
        lanes = lax.broadcasted_iota(jnp.int32, (1, TILE), 1)
        most = [jnp.full((tok, TILE), LOW, jnp.float32) for _ in range(GROUP)]
        for n, t in enumerate(sum(pairs, [])):
            k = kvb[g, t * TILE : (t + 1) * TILE, :HEAD]
            part = lax.dot_general(
                q, k, (((1,), (1,)), ((), ())), preferred_element_type=jnp.float32
            )
            place = lanes + t * TILE
            ok = place >= low
            if (t + 1) * TILE > SPAN * tok:
                ok = ok & (place <= row + SPAN * tok)
            for a in range(GROUP):
                one = jnp.where(ok, part[a * tok : (a + 1) * tok], LOW)
                scores[a * tok : (a + 1) * tok, n * TILE : (n + 1) * TILE] = one
                most[a] = jnp.maximum(most[a], one)
        return [
            jnp.broadcast_to(jnp.max(top, axis=1, keepdims=True), (tok, TILE)) for top in most
        ]

    def score_early(g):
        for a, top in enumerate(score(g, early_pairs)):
            tops[g, a * tok : (a + 1) * tok] = top

    def score_late(g):
        for a, top in enumerate(score(g, late_pairs)):
            r = slice(a * tok, (a + 1) * tok)
            old = tops[g, r]
            top = jnp.maximum(old, top)
            fade[r] = jnp.exp2((old - top) * factor)
            tops[g, r] = top

    def weigh(g, span, acc, pairs):
        ones = jnp.ones((2 * TILE, HEAD), jnp.bfloat16)
        top = tops[g, span]
        n = 0
        for pair in pairs:
            p = []
            for _ in pair:
                part = scores[span, n * TILE : (n + 1) * TILE]
                p.append(jnp.exp2((part - top) * factor).astype(jnp.bfloat16))
                n += 1
            keys = len(pair) * TILE
            v = kvb[g, pair[0] * TILE : pair[0] * TILE + keys, HEAD:]
            v = jnp.concatenate([v, ones[:keys]], axis=1)
            p = jnp.concatenate(p, axis=1)
            acc = acc + jnp.dot(p, v, preferred_element_type=jnp.float32)
        return acc

    def mix_early(g, half):
        span = slice(half * HALF * tok, (half + 1) * HALF * tok)
        zero = jnp.zeros((HALF * tok, 2 * HEAD), jnp.float32)
        sums[g, span] = weigh(g, span, zero, early_pairs)

    def mix_late(g, half):
        span = slice(half * HALF * tok, (half + 1) * HALF * tok)
        old = fade[span]
        acc = sums[g, span] * jnp.concatenate([old, old], axis=1)
        acc = weigh(g, span, acc, late_pairs)
        mean = acc[:, :HEAD] / acc[:, HEAD:]
        big = mean.astype(jnp.bfloat16)
        small = (mean - big.astype(jnp.float32)).astype(jnp.bfloat16)
        back = jnp.dot(big, had, preferred_element_type=jnp.float32) + jnp.dot(
            small, had, preferred_element_type=jnp.float32
        )
        back = (back * scale).astype(jnp.bfloat16)
        for a in range(HALF):
            att[2 * g + half, :, a * HEAD : (a + 1) * HEAD] = back[a * tok : (a + 1) * tok]

    def ship(i):
        return pltpu.make_async_remote_copy(
            src_ref=att.at[i],
            dst_ref=got.at[i],
            send_sem=att_send.at[i],
            recv_sem=att_recv.at[i],
            device_id=after,
            device_id_type=MESH,
        )

    def early_score(g):
        complete(g)
        block(score_early, g)

    def early_mix(g, half):
        block(mix_early, g, half)

    def late_score(g):
        complete_last(g)
        block(score_late, g)

    def late_mix(g, half):
        block(mix_late, g, half)
        ship(2 * g + half).start()

    def turn_queries(i):
        block(rotate_queries, i)

    def near(g):
        onward(g, near_roles)

    def far(g):
        onward(g, far_roles)

    def pairs_on(g):
        onward(g, pair_roles)

    def relays(g):
        onward(g, relay_roles)

    for step in (
        (turn_queries, 0), (pass_on, 0, ZO), (pass_on, 0, PV), (near, 0), (own, 2),
        (turn_queries, 1), (pass_on, 1, ZO), (pass_on, 1, PV), (near, 1), (own, 3),
        (turn_queries, 2), (far, 0), (pass_on, 0, ZP), (pass_on, 2, PV), (near, 2),
        (turn_queries, 3), (pass_on, 2, ZO), (far, 1), (relays, 0), (pairs_on, 0),
        (pass_on, 1, ZP), (pass_on, 3, PV), (near, 3),
        (early_score, 0), (pass_on, 3, ZO), (far, 2), (early_mix, 0, 0), (relays, 1),
        (early_mix, 0, 1), (pairs_on, 1), (pass_on, 2, ZP),
        (early_score, 1), (early_mix, 1, 0), (far, 3), (relays, 2), (early_mix, 1, 1),
        (late_score, 0), (late_mix, 0, 0), (pairs_on, 2), (pass_on, 3, ZP), (late_mix, 0, 1),
        (early_score, 2), (early_mix, 2, 0), (relays, 3), (early_mix, 2, 1),
        (late_score, 1), (late_mix, 1, 0), (pairs_on, 3), (late_mix, 1, 1),
        (early_score, 3), (early_mix, 3, 0), (early_mix, 3, 1),
        (late_score, 2), (late_mix, 2, 0), (late_mix, 2, 1),
        (late_score, 3), (late_mix, 3, 0), (late_mix, 3, 1),
    ):
        step[0](*step[1:])

    for g in range(KEY_VALUE_HEADS):
        drain(g)
    for i in range(2 * KEY_VALUE_HEADS):
        ship(i).wait()


def finish(got_ref, gain_ref, out_ref):
    parts, _, step = got_ref.shape
    x = [got_ref[i].astype(jnp.float32) for i in range(parts)]
    power = sum(jnp.sum(v * v, axis=1, keepdims=True) for v in x) / (parts * step)
    factor = lax.rsqrt(power + 1e-05)
    for i in range(parts):
        out_ref[:, i * step : (i + 1) * step] = (
            x[i] * factor * gain_ref[:, i * step : (i + 1) * step]
        ).astype(jnp.bfloat16)


def solution(mesh):
    planes = mesh.shape["ctx"] // 8
    sections = mesh.shape["segment"]

    def body(queries, key_value_heads, doc_lengths, norm_gain):
        tok = queries.shape[1]
        width = -(-((SPAN + 1) * tok) // 128) * 128
        vmem = pl.BlockSpec(memory_space=pltpu.VMEM)
        bf16, f32 = jnp.bfloat16, jnp.float32
        parts, step = 2 * KEY_VALUE_HEADS, HALF * HEAD
        got = pl.pallas_call(
            functools.partial(kernel, tok, planes, sections),
            out_shape=jax.ShapeDtypeStruct((parts, tok, step), bf16),
            in_specs=[pl.BlockSpec(memory_space=pl.ANY), vmem, vmem],
            out_specs=pl.BlockSpec(memory_space=pl.ANY),
            scratch_shapes=[
                pltpu.VMEM((tok, QUERY_HEADS * HEAD), bf16),
                pltpu.VMEM((KEY_VALUE_HEADS, SLOTS * tok, 2 * HEAD), bf16),
                pltpu.VMEM((QUERY_HEADS * tok, HEAD), bf16),
                pltpu.VMEM((GROUP * tok, width), f32),
                pltpu.VMEM((KEY_VALUE_HEADS, GROUP * tok, 2 * HEAD), f32),
                pltpu.VMEM((KEY_VALUE_HEADS, GROUP * tok, TILE), f32),
                pltpu.VMEM((GROUP * tok, TILE), f32),
                pltpu.VMEM((tok, TILE), jnp.int32),
                pltpu.VMEM((parts, tok, step), bf16),
                pltpu.VMEM((8, 128), jnp.int32),
                pltpu.SemaphoreType.DMA,
                pltpu.SemaphoreType.DMA((KEY_VALUE_HEADS, SENDS)),
                pltpu.SemaphoreType.DMA((KEY_VALUE_HEADS, 10)),
                pltpu.SemaphoreType.DMA((parts,)),
                pltpu.SemaphoreType.DMA((parts,)),
            ],
            compiler_params=pltpu.CompilerParams(
                collective_id=0, has_side_effects=True, vmem_limit_bytes=60 * 2**20
            ),
        )(queries[0], key_value_heads[0], doc_lengths)
        rows = tok // 2 if tok % 16 == 0 else tok
        out = pl.pallas_call(
            finish,
            grid=(tok // rows,),
            out_shape=jax.ShapeDtypeStruct((tok, QUERY_HEADS * HEAD), bf16),
            in_specs=[
                pl.BlockSpec((parts, rows, step), lambda i: (0, i, 0)),
                pl.BlockSpec((1, QUERY_HEADS * HEAD), lambda i: (0, 0)),
            ],
            out_specs=pl.BlockSpec((rows, QUERY_HEADS * HEAD), lambda i: (i, 0)),
        )(got, norm_gain)
        return out[None]

    in_specs = (
        P("segment", "ctx", None),
        P("segment", "ctx", None),
        P("segment", None),
        P("segment", None),
    )
    return jax.shard_map(
        body, mesh=mesh, in_specs=in_specs, out_specs=P("segment", "ctx", None), check_vma=False
    )
```

time: 79.9 us -> 66.7 us (0.83)
  Pallas kernels: 76.9 us -> 66.2 us
  local copies, waits for them, and re-layouts: 2.81 us -> 0 us
    pallas_call x1, Pallas kernels: 76.9 us -> 63.3 us  [body(): pl.pallas_call(functools.partial(kernel, tok, planes, sections), out_shap...]
    pallas_call x0 -> x1, Pallas kernels: none -> 2.92 us  [body(): pl.pallas_call(finish, grid=(tok // rows,), out_shape=jax.ShapeDtypeStruc...]
    unnamed x1 -> x0, local copies, waits for them, and re-layouts: 2.81 us -> none
where the time goes in v2:
time: 66.7 us; the launch traced here: 66.2 us
  Pallas kernels  66.2 us (99%)
    pallas_call x1, Pallas kernels, body(): pl.pallas_call(functools.partial(kernel, tok, planes, sections), out_shap...  63.3 us
    pallas_call x1, Pallas kernels, body(): pl.pallas_call(finish, grid=(tok // rows,), out_shape=jax.ShapeDtypeStruc...  2.92 us

profile of v2, /device:TPU:1, one launch (start us, length us, event | category | flops | bytes accessed | tf_op | source)
XLA Modules:
  0.0 66.2 jit_solution(12934005563944175480)
XLA Ops:
  0.0 63.3 %shard_map.46.got_ref = bf16[8,208,512]{2,1,0:T(8,128)(2,1)} custom-call(bf16[208,4096]{1,0:T(8,128)(2,1)} %bitcast.3, bf16[208,1024]{1,0:T(8,128)(2,1)} %bitcast.4, s32[1,64]{1,0:T(1,128)} %len_ref.1), custom_call_target="tpu_custom_call" | custom-call | tf_op jit(solution)/shard_map/pallas_call | solution.py:418
  63.3 2.9 %shard_map.47 = bf16[208,4096]{1,0:T(8,128)(2,1)} custom-call(bf16[8,208,512]{2,1,0:T(8,128)(2,1)} %shard_map.46.got_ref, f32[1,4096]{1,0:T(1,128)} %gain_ref.1), custom_call_target="tpu_custom_call" | custom-call | tf_op jit(solution)/shard_map/pallas_call | solution.py:445

commit v3 on v2

--- a/solution.py
+++ b/solution.py
@@ -36,9 +36,9 @@
 
 def kernel(
     tok, planes, sections,
-    q_hbm, kv_ref, len_ref, got,
-    q_ref, kvb, qr, scores, sums, tops, fade, tri, att, lens,
-    q_sem, send_sem, recv_sem, att_send, att_recv,
+    q_hbm, kv_hbm, len_ref, got,
+    q_ref, kv_ref, kvb, qr, scores, sums, tops, fade, tri, att, lens,
+    q_sem, kv_sem, send_sem, recv_sem, att_send, att_recv,
 ):
     width = -(-((SPAN + 1) * tok) // 128) * 128
     scale = HEAD ** (-0.5)
@@ -64,6 +64,8 @@
     after = {"segment": lax.rem(s + 1, sections)}
     before = {"segment": lax.rem(s + sections - 1, sections)}
 
+    kv_copy = pltpu.make_async_copy(kv_hbm, kv_ref, kv_sem)
+    kv_copy.start()
     q_copy = pltpu.make_async_copy(q_hbm, q_ref, q_sem)
     q_copy.start()
     barrier = pltpu.get_barrier_semaphore()
@@ -217,6 +219,7 @@
             kv_ref[:, (KEY_VALUE_HEADS + g) * HEAD : (KEY_VALUE_HEADS + g + 1) * HEAD]
         )
 
+    kv_copy.wait()
     block(rotate, 0)
     block(rotate, 1)
     pl.semaphore_wait(barrier, 7)
@@ -376,12 +379,12 @@
         (turn_queries, 2), (far, 0), (pass_on, 0, ZP), (pass_on, 2, PV), (near, 2),
         (turn_queries, 3), (pass_on, 2, ZO), (far, 1), (relays, 0), (pairs_on, 0),
         (pass_on, 1, ZP), (pass_on, 3, PV), (near, 3),
-        (early_score, 0), (pass_on, 3, ZO), (far, 2), (early_mix, 0, 0), (relays, 1),
+        (early_score, 0), (pass_on, 3, ZO), (early_mix, 0, 0), (far, 2), (relays, 1),
         (early_mix, 0, 1), (pairs_on, 1), (pass_on, 2, ZP),
-        (early_score, 1), (early_mix, 1, 0), (far, 3), (relays, 2), (early_mix, 1, 1),
-        (late_score, 0), (late_mix, 0, 0), (pairs_on, 2), (pass_on, 3, ZP), (late_mix, 0, 1),
-        (early_score, 2), (early_mix, 2, 0), (relays, 3), (early_mix, 2, 1),
-        (late_score, 1), (late_mix, 1, 0), (pairs_on, 3), (late_mix, 1, 1),
+        (early_score, 1), (early_mix, 1, 0), (relays, 2), (early_mix, 1, 1),
+        (late_score, 0), (late_mix, 0, 0), (far, 3), (pairs_on, 2), (pass_on, 3, ZP), (late_mix, 0, 1),
+        (early_score, 2), (early_mix, 2, 0), (early_mix, 2, 1),
+        (late_score, 1), (late_mix, 1, 0), (relays, 3), (pairs_on, 3), (late_mix, 1, 1),
         (early_score, 3), (early_mix, 3, 0), (early_mix, 3, 1),
         (late_score, 2), (late_mix, 2, 0), (late_mix, 2, 1),
         (late_score, 3), (late_mix, 3, 0), (late_mix, 3, 1),
@@ -418,10 +421,11 @@
         got = pl.pallas_call(
             functools.partial(kernel, tok, planes, sections),
             out_shape=jax.ShapeDtypeStruct((parts, tok, step), bf16),
-            in_specs=[pl.BlockSpec(memory_space=pl.ANY), vmem, vmem],
+            in_specs=[pl.BlockSpec(memory_space=pl.ANY), pl.BlockSpec(memory_space=pl.ANY), vmem],
             out_specs=pl.BlockSpec(memory_space=pl.ANY),
             scratch_shapes=[
                 pltpu.VMEM((tok, QUERY_HEADS * HEAD), bf16),
+                pltpu.VMEM((tok, 2 * KEY_VALUE_HEADS * HEAD), bf16),
                 pltpu.VMEM((KEY_VALUE_HEADS, SLOTS * tok, 2 * HEAD), bf16),
                 pltpu.VMEM((QUERY_HEADS * tok, HEAD), bf16),
                 pltpu.VMEM((GROUP * tok, width), f32),
@@ -431,6 +435,7 @@
                 pltpu.VMEM((tok, TILE), jnp.int32),
                 pltpu.VMEM((parts, tok, step), bf16),
                 pltpu.VMEM((8, 128), jnp.int32),
+                pltpu.SemaphoreType.DMA,
                 pltpu.SemaphoreType.DMA,
                 pltpu.SemaphoreType.DMA((KEY_VALUE_HEADS, SENDS)),
                 pltpu.SemaphoreType.DMA((KEY_VALUE_HEADS, 10)),

time: 66.7 us -> 65.2 us (0.978)
  Pallas kernels: 66.2 us -> 64.3 us
    pallas_call x1, Pallas kernels: 63.3 us -> 61.4 us  [body(): pl.pallas_call(functools.partial(kernel, tok, planes, sections), out_shap...]
where the time goes in v3:
time: 65.2 us; the launch traced here: 64.3 us
  Pallas kernels  64.3 us (99%)
    pallas_call x1, Pallas kernels, body(): pl.pallas_call(functools.partial(kernel, tok, planes, sections), out_shap...  61.4 us
    pallas_call x1, Pallas kernels, body(): pl.pallas_call(finish, grid=(tok // rows,), out_shape=jax.ShapeDtypeStruc...  2.92 us

profile of v3, /device:TPU:1, one launch (start us, length us, event | category | flops | bytes accessed | tf_op | source)
XLA Modules:
  0.0 64.3 jit_solution(7540279363198526619)
XLA Ops:
  0.0 61.4 %shard_map.46.got_ref = bf16[8,208,512]{2,1,0:T(8,128)(2,1)} custom-call(bf16[208,4096]{1,0:T(8,128)(2,1)} %bitcast.3, bf16[208,1024]{1,0:T(8,128)(2,1)} %bitcast.4, s32[1,64]{1,0:T(1,128)} %len_ref.1), custom_call_target="tpu_custom_call" | custom-call | tf_op jit(solution)/shard_map/pallas_call | solution.py:421
  61.4 2.9 %shard_map.47 = bf16[208,4096]{1,0:T(8,128)(2,1)} custom-call(bf16[8,208,512]{2,1,0:T(8,128)(2,1)} %shard_map.46.got_ref, f32[1,4096]{1,0:T(1,128)} %gain_ref.1), custom_call_target="tpu_custom_call" | custom-call | tf_op jit(solution)/shard_map/pallas_call | solution.py:450
